TPU v7x, 128 devices: a whole 4x4x4 slice. The times are simulated.
128 devices in a mesh: ctx: 8 (over y_hi, z), exp: 16 (over y_lo, x, core).
Axes of the slice: x: 4, y: 4 (y_hi: 2, y_lo: 2; y = y_hi * 2 + y_lo), z: 4, core: 2. Of those that a mesh axis runs over, the one named last changes fastest.
Arguments:
- moe_input: bfloat16 [16384, 4096], P(('ctx', 'exp')), may hold values from -6 to 6
- out_grad: bfloat16 [16384, 4096], P(('ctx', 'exp')), may hold values from -6 to 6
- w_gate: bfloat16 [32, 4096, 1408], P('exp', None, 'ctx'), may hold values from -0.09375 to 0.09375
- w_up: bfloat16 [32, 4096, 1408], P('exp', None, 'ctx'), may hold values from -0.09375 to 0.09375
- w_down: bfloat16 [32, 1408, 4096], P('exp', 'ctx'), may hold values from -0.15625 to 0.15625
- expert_picks: int32 [32, 128], replicated, may hold values from 0 to 16383, as said below
- gate_probs: float32 [32, 128], replicated, may hold values from 0.2 to 1
- queries: bfloat16 [16384, 2048], P('ctx', 'exp'), may hold values from -6 to 6
- attn_keys: bfloat16 [16384, 2048], P('ctx', 'exp'), may hold values from -6 to 6
- values: bfloat16 [16384, 2048], P('ctx', 'exp'), may hold values from -6 to 6
- attn_out: bfloat16 [16384, 2048], P('ctx', 'exp'), may hold values from -1.5 to 1.5
- log_norm: float32 [16, 16384], P('exp'), may hold values from -1 to 12
- w_out: bfloat16 [2048, 4096], P('exp'), may hold values from -0.09375 to 0.09375
Outputs:
- d_resid: bfloat16 [16384, 4096], P(('ctx', 'exp'))
- dw_gate: bfloat16 [32, 4096, 1408], P('exp', None, 'ctx')
- dw_up: bfloat16 [32, 4096, 1408], P('exp', None, 'ctx')
- dw_down: bfloat16 [32, 1408, 4096], P('exp', 'ctx')
- d_gates: float32 [32, 128], P('exp', 'ctx')
- dw_out: bfloat16 [2048, 4096], P('exp', 'ctx')
- grad_q: bfloat16 [16384, 2048], P('ctx', 'exp')
- grad_k: bfloat16 [16384, 2048], P('ctx', 'exp')
- grad_v: bfloat16 [16384, 2048], P('ctx', 'exp')
Inputs may be any that keep to these rules, and one draw needn't show every extreme that they name: expert_picks[e] lists distinct tokens in ascending order: exactly 16 from each context group of 2048 consecutive tokens and at most 2 from each aligned block of 128 tokens; in every group some block gives exactly 2.
All inputs are finite; a program needn't handle non-finite values.
Results may differ from a plain program's by a relative error of at most 0.023.
Values may be sent and summed in bfloat16 or wider, within the bound.
A program may use at most 256 MiB of HBM per device.

v0:
```python
import math
import jax
import jax.numpy as jnp
from jax import lax
from jax.sharding import PartitionSpec as P

MOST = 2


def activation(pre_act):
    sigmoid_val = jax.nn.sigmoid(pre_act)
    return (pre_act * sigmoid_val, sigmoid_val * (1.0 + pre_act * (1.0 - sigmoid_val)))


def settle(value):
    return lax.optimization_barrier(value.astype(jnp.bfloat16)).astype(jnp.float32)


def contract_first(left, right):
    return lax.dot_general(
        left, right, (((0,), (0,)), ((), ())), preferred_element_type=jnp.float32
    )


def contract_last(left, right):
    return lax.dot_general(
        left, right, (((1,), (1,)), ((), ())), preferred_element_type=jnp.float32
    )


def tile_grads(
    q_rows, do_rows, norm_rows, delta_rows, keys_here, values_here, key_pos, key_scale, piece_count
):
    row_count, head_dim = q_rows.shape
    block_rows = math.gcd(row_count, 2048)
    block_total = row_count // block_rows
    piece_len = keys_here.shape[0] // piece_count

    def one_block(block_idx, carried):
        grad_rows, grad_keys, grad_values = carried
        row_start = block_idx * block_rows
        q_block = lax.dynamic_slice_in_dim(q_rows, row_start, block_rows, 0)
        do_block = lax.dynamic_slice_in_dim(do_rows, row_start, block_rows, 0)
        norm_block = lax.dynamic_slice_in_dim(norm_rows, row_start, block_rows, 0)
        delta_block = lax.dynamic_slice_in_dim(delta_rows, row_start, block_rows, 0)
        q_positions = row_start + jnp.arange(block_rows, dtype=jnp.int32)
        last_query = row_start + block_rows - 1
        keys_piece = keys_here
        values_piece = values_here
        pos_piece = key_pos

        def compute_tile(
            unused, keys_piece=keys_piece, values_piece=values_piece, pos_piece=pos_piece
        ):
            scores = contract_last(q_block, keys_piece) * key_scale
            causal = pos_piece[None, :] <= q_positions[:, None]
            attn_probs = jnp.exp(jnp.where(causal, scores - norm_block[:, None], -1e30))
            d_probs = contract_last(do_block, values_piece)
            d_scores = (attn_probs * (d_probs - delta_block[:, None])).astype(jnp.bfloat16)
            probs_low = attn_probs.astype(jnp.bfloat16)
            piece_q = jnp.dot(d_scores, keys_piece, preferred_element_type=jnp.float32) * key_scale
            piece_k = contract_first(d_scores, q_block) * key_scale
            piece_v = contract_first(probs_low, do_block)
            return (piece_q, piece_k, piece_v)

        def skip_tile(unused):
            return (
                jnp.zeros((block_rows, head_dim), jnp.float32),
                jnp.zeros((piece_len, head_dim), jnp.float32),
                jnp.zeros((piece_len, head_dim), jnp.float32),
            )

        piece_q, piece_k, piece_v = lax.cond(
            last_query >= jnp.min(pos_piece), compute_tile, skip_tile, 0
        )
        key_parts = [piece_k]
        value_parts = [piece_v]
        add_k = jnp.concatenate(key_parts, axis=0)
        add_v = jnp.concatenate(value_parts, axis=0)
        grad_rows = lax.dynamic_update_slice_in_dim(grad_rows, piece_q, row_start, 0)
        return (grad_rows, grad_keys + add_k, grad_values + add_v)

    start_state = (
        jnp.zeros((row_count, head_dim), jnp.float32),
        jnp.zeros(keys_here.shape, jnp.float32),
        jnp.zeros(values_here.shape, jnp.float32),
    )
    return lax.fori_loop(0, block_total, one_block, start_state)


def body(
    moe_input,
    out_grad,
    w_gate,
    w_up,
    w_down,
    expert_picks,
    gate_probs,
    queries,
    attn_keys,
    values,
    attn_out,
    log_norm,
    w_out,
):
    n_ctx = lax.axis_size("ctx")
    n_exp = lax.axis_size("exp")
    ctx_id = lax.axis_index("ctx")
    exp_id = lax.axis_index("exp")
    tok_dev, feat_width = moe_input.shape
    n_local = w_gate.shape[0]
    slot_count = MOST
    group_picks = expert_picks.shape[1] // n_ctx
    block_id = ctx_id * n_exp + exp_id
    base_row = block_id * tok_dev
    count_below = jnp.sum((expert_picks < base_row).astype(jnp.int32), axis=1)
    inside = jnp.sum(
        ((expert_picks >= base_row) & (expert_picks < base_row + tok_dev)).astype(jnp.int32), axis=1
    )
    offsets = jnp.arange(slot_count, dtype=jnp.int32)
    slot_spots = jnp.minimum(count_below[:, None] + offsets[None, :], expert_picks.shape[1] - 1)
    is_valid = offsets[None, :] < inside[:, None]
    chosen = jnp.where(
        is_valid, jnp.take_along_axis(expert_picks, slot_spots, axis=1) - base_row, 0
    )
    send_rows = jnp.where(is_valid[..., None], moe_input[chosen], jnp.zeros((), jnp.bfloat16))
    send_grads = jnp.where(is_valid[..., None], out_grad[chosen], jnp.zeros((), jnp.bfloat16))
    got_rows, got_grads = (
        lax.all_to_all(
            send_rows.reshape(n_exp, n_local, slot_count, feat_width),
            "exp",
            split_axis=0,
            concat_axis=0,
            tiled=True,
        ),
        lax.all_to_all(
            send_grads.reshape(n_exp, n_local, slot_count, feat_width),
            "exp",
            split_axis=0,
            concat_axis=0,
            tiled=True,
        ),
    )
    my_picks = lax.dynamic_slice(
        expert_picks, (exp_id * n_local, ctx_id * group_picks), (n_local, group_picks)
    )
    src_exp = my_picks // tok_dev - ctx_id * n_exp
    starts = my_picks // tok_dev * tok_dev
    slot_rank = jnp.arange(group_picks, dtype=jnp.int32)[None, :] - jnp.sum(
        (my_picks[:, None, :] < starts[:, :, None]).astype(jnp.int32), axis=2
    )
    flat_pos = (
        (src_exp * n_local + jnp.arange(n_local, dtype=jnp.int32)[:, None]) * slot_count + slot_rank
    ).reshape(-1)
    mine_rows = jnp.take(got_rows.reshape(-1, feat_width), flat_pos, axis=0).reshape(
        n_local, group_picks, feat_width
    )
    mine_grads = jnp.take(got_grads.reshape(-1, feat_width), flat_pos, axis=0).reshape(
        n_local, group_picks, feat_width
    )
    slot_rows, slot_grads = (
        lax.all_gather(mine_rows, "ctx", axis=1, tiled=True),
        lax.all_gather(mine_grads, "ctx", axis=1, tiled=True),
    )
    gate_rows = lax.dynamic_slice_in_dim(gate_probs, exp_id * n_local, n_local, 0)
    pre_gate = jnp.einsum("kcd,kdf->kcf", slot_rows, w_gate, preferred_element_type=jnp.float32)
    pre_up = jnp.einsum("kcd,kdf->kcf", slot_rows, w_up, preferred_element_type=jnp.float32)
    gated_act, act_slope = activation(pre_gate)
    hidden_full = gated_act * pre_up
    hidden = hidden_full.astype(jnp.bfloat16)
    down_back = jnp.einsum("kcd,kfd->kcf", slot_grads, w_down, preferred_element_type=jnp.float32)
    gate_part = settle(jnp.sum(down_back * hidden_full, axis=2))
    scaled = gate_rows[..., None] * down_back
    d_gate = (scaled * pre_up * act_slope).astype(jnp.bfloat16)
    d_up = (scaled * gated_act).astype(jnp.bfloat16)
    weighted = (gate_rows[..., None] * slot_grads.astype(jnp.float32)).astype(jnp.bfloat16)
    dw_down = jnp.einsum(
        "kcf,kcd->kfd", hidden, weighted, preferred_element_type=jnp.float32
    ).astype(jnp.bfloat16)
    dw_gate = jnp.einsum(
        "kcd,kcf->kdf", slot_rows, d_gate, preferred_element_type=jnp.float32
    ).astype(jnp.bfloat16)
    dw_up = jnp.einsum("kcd,kcf->kdf", slot_rows, d_up, preferred_element_type=jnp.float32).astype(
        jnp.bfloat16
    )
    dx_part = settle(
        jnp.einsum("kcf,kdf->kcd", d_gate, w_gate, preferred_element_type=jnp.float32)
        + jnp.einsum("kcf,kdf->kcd", d_up, w_up, preferred_element_type=jnp.float32)
    )
    dx_sum, d_gates = (
        lax.psum_scatter(
            dx_part.astype(jnp.bfloat16), "ctx", scatter_dimension=1, tiled=True
        ).astype(jnp.float32),
        lax.psum_scatter(
            gate_part.astype(jnp.bfloat16), "ctx", scatter_dimension=1, tiled=True
        ).astype(jnp.float32),
    )
    dx_slot = dx_sum.astype(jnp.bfloat16)
    back_rows = (
        jnp.zeros((n_exp * n_local * slot_count, feat_width), jnp.bfloat16)
        .at[flat_pos]
        .set(dx_slot.reshape(-1, feat_width))
    )
    returned = lax.all_to_all(
        back_rows.reshape(n_exp, n_local, slot_count, feat_width),
        "exp",
        split_axis=0,
        concat_axis=0,
        tiled=True,
    )
    returned = returned.reshape(-1, feat_width)
    onehot = (
        (chosen.reshape(-1)[None, :] == jnp.arange(tok_dev, dtype=jnp.int32)[:, None])
        & is_valid.reshape(-1)[None, :]
    ).astype(jnp.bfloat16)
    d_resid = (
        out_grad.astype(jnp.float32) + jnp.dot(onehot, returned, preferred_element_type=jnp.float32)
    ).astype(jnp.bfloat16)
    tok_ctx, head_dim = queries.shape
    key_scale = head_dim ** (-0.5)
    piece_rows = lax.all_gather(d_resid, "exp", axis=0, tiled=True)
    out_rows = contract_last(piece_rows, w_out)
    d_out_acc = out_rows.astype(jnp.bfloat16)
    dw_part = contract_first(attn_out, piece_rows)
    d_out, dw_part = (d_out_acc, dw_part)
    dw_out = lax.psum_scatter(
        settle(dw_part).astype(jnp.bfloat16), "ctx", scatter_dimension=1, tiled=True
    )
    row_delta = jnp.sum(d_out.astype(jnp.float32) * attn_out.astype(jnp.float32), axis=1)
    lse_all = log_norm[0]
    keys_here, values_here = (attn_keys, values)
    key_pos = ctx_id * tok_ctx + jnp.arange(tok_ctx, dtype=jnp.int32)
    key_pieces = 1
    delta_all = lax.all_gather(row_delta, "ctx", axis=0, tiled=True)
    q_rows = lax.all_gather(queries, "ctx", axis=0, tiled=True)
    do_rows = lax.all_gather(d_out, "ctx", axis=0, tiled=True)
    add_q, add_k, add_v = tile_grads(
        q_rows, do_rows, lse_all, delta_all, keys_here, values_here, key_pos, key_scale, key_pieces
    )
    dq_all = add_q
    dq_all, grad_keys, grad_values = (dq_all, add_k, add_v)
    grad_q = lax.psum_scatter(dq_all.astype(jnp.bfloat16), "ctx", scatter_dimension=0, tiled=True)
    grad_k = grad_keys.astype(jnp.bfloat16)
    grad_v = grad_values.astype(jnp.bfloat16)
    return (d_resid, dw_gate, dw_up, dw_down, d_gates, dw_out, grad_q, grad_k, grad_v)


def solution(mesh):
    return jax.shard_map(
        body,
        mesh=mesh,
        in_specs=(
            P(("ctx", "exp"), None),
            P(("ctx", "exp"), None),
            P("exp", None, "ctx"),
            P("exp", None, "ctx"),
            P("exp", "ctx", None),
            P(),
            P(),
            P("ctx", "exp"),
            P("ctx", "exp"),
            P("ctx", "exp"),
            P("ctx", "exp"),
            P("exp", None),
            P("exp", None),
        ),
        out_specs=(
            P(("ctx", "exp"), None),
            P("exp", None, "ctx"),
            P("exp", None, "ctx"),
            P("exp", "ctx", None),
            P("exp", "ctx"),
            P("exp", "ctx"),
            P("ctx", "exp"),
            P("ctx", "exp"),
            P("ctx", "exp"),
        ),
        check_vma=False,
    )
```

profile of v0, /device:TPU:0, one launch (start us, length us, event | category | flops | bytes accessed | tf_op | source)
XLA Modules:
  0.0 887.2 jit_solution(8527836403347974611)
XLA Ops:
  26.4 10.5 %all-to-all-done = bf16[16,2,2,4096]{3,2,1,0:T(2,128)(2,1)S(1)} async-done(((bf16[16,2,2,4096]{3,2,1,0:T(2,128)(2,1)}), bf16[16,2,2,4096]{3,2,1,0:T(2,128)(2,1)S(1)}, u32[]{:S(2)}, u32[]{:S(2)}) %all-to-all-start) | async-done | bytes 524320 | tf_op jit(solution)/shard_map/all_to_all | solution.py:136
  58.2 52.4 %all-gather.8.cloned.1.call-done = bf16[2,128,4096]{2,1,0:T(8,128)(2,1)} async-done(((bf16[2,16,4096]{2,1,0:T(8,128)(2,1)}), bf16[2,128,4096]{2,1,0:T(8,128)(2,1)}) %all-gather.8.cloned.1.call-update) | async-done | bytes 2097168 | tf_op jit(solution)/shard_map/all_gather | solution.py:162
  114.6 50.8 %all-gather.6.cloned.1.call-done = bf16[2,128,4096]{2,1,0:T(8,128)(2,1)} async-done(((bf16[2,16,4096]{2,1,0:T(8,128)(2,1)}), bf16[2,128,4096]{2,1,0:T(8,128)(2,1)}) %all-gather.6.cloned.1.call-update) | async-done | bytes 2097168 | tf_op jit(solution)/shard_map/all_gather | solution.py:163
  172.9 73.0 %reduce-scatter.7.cloned.1.call-done = bf16[2,16,4096]{2,1,0:T(8,128)(2,1)} async-done(((bf16[2,128,4096]{2,1,0:T(8,128)(2,1)}), bf16[2,16,4096]{2,1,0:T(8,128)(2,1)}) %reduce-scatter.7.cloned.1.call-update) | async-done | bytes 262160 | tf_op jit(solution)/shard_map/reduce_scatter | solution.py:191
  253.9 9.9 %all-to-all-done.2 = bf16[16,2,2,4096]{3,2,1,0:T(2,128)(2,1)S(1)} async-done(((bf16[16,2,2,4096]{3,2,1,0:T(2,128)(2,1)}), bf16[16,2,2,4096]{3,2,1,0:T(2,128)(2,1)S(1)}, u32[]{:S(2)}, u32[]{:S(2)}) %all-to-all-start.2) | async-done | bytes 524320 | tf_op jit(solution)/shard_map/all_to_all | solution.py:204
  265.7 88.6 %all-gather.10.cloned.1.call-done = bf16[2048,4096]{1,0:T(8,128)(2,1)} async-done(((bf16[128,4096]{1,0:T(8,128)(2,1)}), bf16[2048,4096]{1,0:T(8,128)(2,1)}) %all-gather.10.cloned.1.call-update) | async-done | bytes 16777232 | tf_op jit(solution)/shard_map/all_gather | solution.py:221
  354.4 12.4 %multiply_reduce_fusion = (f32[2048]{0:T(1024)S(1)}, bf16[2048,128]{0,1:T(8,128)(2,1)}) fusion(bf16[2048,128]{0,1:T(8,128)(2,1)S(1)} %copy.31, bf16[2048,4096]{1,0:T(8,128)(2,1)} %all-gather.10.cloned.1.call-done, bf16[128,4096]{1,0:T(8,128)(2,1)} %param.31), kind=kOutput, calls=%fused_computation.41 | convolution fusion | flops 2148792320 | bytes 18882560 | tf_op jit(solution)/shard_map/dot_general | solution.py:26
  368.9 9.2 %fusion.18 = bf16[128,4096]{0,1:T(8,128)(2,1)} fusion(bf16[2048,4096]{1,0:T(8,128)(2,1)} %all-gather.10.cloned.1.call-done, bf16[2048,128]{1,0:T(8,128)(2,1)S(1)} %copy-done.16), kind=kOutput, calls=%fused_computation.37 | convolution fusion | flops 2148007936 | bytes 18350080 | tf_op jit(solution)/shard_map/dot_general | solution.py:20
  378.1 36.5 %all_gather.23 = f32[16384]{0:T(1024)} all-gather(f32[2048]{0:T(1024)S(1)} %get-tuple-element.634), channel_id=1, replica_groups=mesh['ctx'=8,'exp'=16] {'ctx'}, dimensions={0}, use_global_device_ids=true | all-gather | bytes 73728 | tf_op jit(solution)/shard_map/all_gather | solution.py:234
  414.7 24.9 %all-gather.14.cloned.1.call-done = bf16[16384,128]{0,1:T(8,128)(2,1)} async-done(((bf16[2048,128]{0,1:T(8,128)(2,1)}), bf16[16384,128]{0,1:T(8,128)(2,1)}) %all-gather.14.cloned.1.call-update) | async-done | bytes 4194320 | tf_op jit(solution)/shard_map/all_gather | solution.py:236
  446.0 65.2 %all-gather.12.cloned.1.call-done = bf16[16384,128]{1,0:T(8,128)(2,1)} async-done(((bf16[2048,128]{1,0:T(8,128)(2,1)}), bf16[16384,128]{1,0:T(8,128)(2,1)}) %all-gather.12.cloned.1.call-update) | async-done | bytes 4194320 | tf_op jit(solution)/shard_map/all_gather | solution.py:235
  513.4 285.8 %while.22 = (s32[]{:T(128)}, bf16[16384,128]{1,0:T(8,128)(2,1)}, f32[2048,128]{1,0:T(8,128)}, f32[2048,128]{1,0:T(8,128)}, s32[]{:T(128)}, /*index=5*/bf16[16384...) while((s32[]{:T(128)}, bf16[16384,128]{1,0:T(8,128)(2,1)}, ...), condition=%wide.region_13.15_spmd.clone, body=%wide.region_10.14_spmd.clone.sunk | while | flops 5420617728 | bytes 126487464 | solution.py:88
  524.2 28.8 %conditional.3 = (f32[2048,128]{1,0:T(8,128)}, f32[2048,128]{1,0:T(8,128)S(1)}, f32[2048,128]{1,0:T(8,128)S(1)}) conditional(s32[]{:T(128)} %convert_element_type.156, () %tuple.94, (s32[]{:T(128)}, s32[]{:T(128)}, s32[2048]{0:T(1024)S(1)}, bf16[16384,128]{1,0:T(8,128)(2,1)}, s32[]{:T(128)}, /*index=5*/bf16[2048,128]{1,0:T(8,128)(2,1)S(1)}, ...), branch_computations={%region_11.12_spmd, %region_12.13_spmd} | conditional | flops 5419569152 | bytes 118089824 | solution.py:73
  535.2 8.3 multiply_convert_fusion
  557.4 28.7 %conditional.3 = (f32[2048,128]{1,0:T(8,128)}, f32[2048,128]{1,0:T(8,128)S(1)}, f32[2048,128]{1,0:T(8,128)S(1)}) conditional(s32[]{:T(128)} %convert_element_type.156, () %tuple.94, (s32[]{:T(128)}, s32[]{:T(128)}, s32[2048]{0:T(1024)S(1)}, bf16[16384,128]{1,0:T(8,128)(2,1)}, s32[]{:T(128)}, /*index=5*/bf16[2048,128]{1,0:T(8,128)(2,1)S(1)}, ...), branch_computations={%region_11.12_spmd, %region_12.13_spmd} | conditional | flops 5419569152 | bytes 118089824 | solution.py:73
  592.0 28.8 %conditional.3 = (f32[2048,128]{1,0:T(8,128)}, f32[2048,128]{1,0:T(8,128)S(1)}, f32[2048,128]{1,0:T(8,128)S(1)}) conditional(s32[]{:T(128)} %convert_element_type.156, () %tuple.94, (s32[]{:T(128)}, s32[]{:T(128)}, s32[2048]{0:T(1024)S(1)}, bf16[16384,128]{1,0:T(8,128)(2,1)}, s32[]{:T(128)}, /*index=5*/bf16[2048,128]{1,0:T(8,128)(2,1)S(1)}, ...), branch_computations={%region_11.12_spmd, %region_12.13_spmd} | conditional | flops 5419569152 | bytes 118089824 | solution.py:73
  626.7 28.8 %conditional.3 = (f32[2048,128]{1,0:T(8,128)}, f32[2048,128]{1,0:T(8,128)S(1)}, f32[2048,128]{1,0:T(8,128)S(1)}) conditional(s32[]{:T(128)} %convert_element_type.156, () %tuple.94, (s32[]{:T(128)}, s32[]{:T(128)}, s32[2048]{0:T(1024)S(1)}, bf16[16384,128]{1,0:T(8,128)(2,1)}, s32[]{:T(128)}, /*index=5*/bf16[2048,128]{1,0:T(8,128)(2,1)S(1)}, ...), branch_computations={%region_11.12_spmd, %region_12.13_spmd} | conditional | flops 5419569152 | bytes 118089824 | solution.py:73
  637.7 8.3 multiply_convert_fusion
  661.4 28.7 %conditional.3 = (f32[2048,128]{1,0:T(8,128)}, f32[2048,128]{1,0:T(8,128)S(1)}, f32[2048,128]{1,0:T(8,128)S(1)}) conditional(s32[]{:T(128)} %convert_element_type.156, () %tuple.94, (s32[]{:T(128)}, s32[]{:T(128)}, s32[2048]{0:T(1024)S(1)}, bf16[16384,128]{1,0:T(8,128)(2,1)}, s32[]{:T(128)}, /*index=5*/bf16[2048,128]{1,0:T(8,128)(2,1)S(1)}, ...), branch_computations={%region_11.12_spmd, %region_12.13_spmd} | conditional | flops 5419569152 | bytes 118089824 | solution.py:73
  672.4 8.3 multiply_convert_fusion
  696.0 28.7 %conditional.3 = (f32[2048,128]{1,0:T(8,128)}, f32[2048,128]{1,0:T(8,128)S(1)}, f32[2048,128]{1,0:T(8,128)S(1)}) conditional(s32[]{:T(128)} %convert_element_type.156, () %tuple.94, (s32[]{:T(128)}, s32[]{:T(128)}, s32[2048]{0:T(1024)S(1)}, bf16[16384,128]{1,0:T(8,128)(2,1)}, s32[]{:T(128)}, /*index=5*/bf16[2048,128]{1,0:T(8,128)(2,1)S(1)}, ...), branch_computations={%region_11.12_spmd, %region_12.13_spmd} | conditional | flops 5419569152 | bytes 118089824 | solution.py:73
  730.6 28.7 %conditional.3 = (f32[2048,128]{1,0:T(8,128)}, f32[2048,128]{1,0:T(8,128)S(1)}, f32[2048,128]{1,0:T(8,128)S(1)}) conditional(s32[]{:T(128)} %convert_element_type.156, () %tuple.94, (s32[]{:T(128)}, s32[]{:T(128)}, s32[2048]{0:T(1024)S(1)}, bf16[16384,128]{1,0:T(8,128)(2,1)}, s32[]{:T(128)}, /*index=5*/bf16[2048,128]{1,0:T(8,128)(2,1)S(1)}, ...), branch_computations={%region_11.12_spmd, %region_12.13_spmd} | conditional | flops 5419569152 | bytes 118089824 | solution.py:73
  765.2 28.7 %conditional.3 = (f32[2048,128]{1,0:T(8,128)}, f32[2048,128]{1,0:T(8,128)S(1)}, f32[2048,128]{1,0:T(8,128)S(1)}) conditional(s32[]{:T(128)} %convert_element_type.156, () %tuple.94, (s32[]{:T(128)}, s32[]{:T(128)}, s32[2048]{0:T(1024)S(1)}, bf16[16384,128]{1,0:T(8,128)(2,1)}, s32[]{:T(128)}, /*index=5*/bf16[2048,128]{1,0:T(8,128)(2,1)S(1)}, ...), branch_computations={%region_11.12_spmd, %region_12.13_spmd} | conditional | flops 5419569152 | bytes 118089824 | solution.py:73
  815.5 64.9 %reduce-scatter.11.cloned.1.call-done = bf16[2048,128]{1,0:T(8,128)(2,1)} async-done(((bf16[16384,128]{1,0:T(8,128)(2,1)}), bf16[2048,128]{1,0:T(8,128)(2,1)}) %reduce-scatter.11.cloned.1.call-update) | async-done | bytes 524304 | tf_op jit(solution)/shard_map/reduce_scatter | solution.py:242
  (248 shorter events, 333.6 us)
Async XLA Ops:
  7.2 103.4 %copy-start = (bf16[2,4096,176]{1,2,0:T(8,128)(2,1)S(1)}, bf16[2,4096,176]{1,2,0:T(8,128)(2,1)}, u32[]{:S(2)}) copy-start(bf16[2,4096,176]{1,2,0:T(8,128)(2,1)} %param.21) | copy-start | bytes 8650756
  20.6 16.4 %all-to-all-start = ((bf16[16,2,2,4096]{3,2,1,0:T(2,128)(2,1)}), bf16[16,2,2,4096]{3,2,1,0:T(2,128)(2,1)S(1)}, u32[]{:S(2)}, u32[]{:S(2)}) async-start(bf16[16,2,2,4096]{3,2,1,0:T(2,128)(2,1)} %get-tuple-element.630), calls=%async_computation | async-start | bytes 1048576 | tf_op jit(solution)/shard_map/all_to_all | solution.py:136
  36.9 15.1 %all-to-all-start.1 = ((bf16[16,2,2,4096]{3,2,1,0:T(2,128)(2,1)}), bf16[16,2,2,4096]{3,2,1,0:T(2,128)(2,1)}, u32[]{:S(2)}, u32[]{:S(2)}) async-start(bf16[16,2,2,4096]{3,2,1,0:T(2,128)(2,1)} %get-tuple-element.631), calls=%async_computation.1 | async-start | bytes 1048576 | tf_op jit(solution)/shard_map/all_to_all | solution.py:129
  41.2 69.4 %all-gather.8.cloned.1.call-start = ((), (), s32[]{:S(2)}) async-start(), calls=%async_computation.8 | async-start | bytes 2359296 | tf_op jit(solution)/shard_map/all_gather | solution.py:162
  56.7 108.7 %all-gather.6.cloned.1.call-start = ((), (), s32[]{:S(2)}) async-start(), calls=%async_computation.7 | async-start | bytes 2359296 | tf_op jit(solution)/shard_map/all_gather | solution.py:163
  57.4 188.5 %reduce-scatter.7.cloned.1.call-start = ((), (), s32[]{:S(2)}) async-start(), calls=%async_computation.9 | async-start | bytes 2359296 | tf_op jit(solution)/shard_map/reduce_scatter | solution.py:191
  58.2 107.2 %copy-start.21 = (f32[2,128]{1,0:T(2,128)}, f32[2,128]{1,0:T(2,128)S(1)}, u32[]{:S(2)}) copy-start(f32[2,128]{1,0:T(2,128)S(1)} %constant_dynamic-slice_fusion) | copy-start | bytes 3076
  113.7 55.1 %copy-start.12 = (f32[2,128,176]{1,2,0:T(8,128)}, f32[2,128,176]{1,2,0:T(8,128)S(1)}, u32[]{:S(2)}) copy-start(f32[2,128,176]{1,2,0:T(8,128)S(1)} %fusion.35) | copy-start | bytes 540676
  114.6 55.0 %copy-start.14 = (f32[2,128,176]{1,2,0:T(8,128)}, f32[2,128,176]{1,2,0:T(8,128)S(1)}, u32[]{:S(2)}) copy-start(f32[2,128,176]{1,2,0:T(8,128)S(1)} %fusion.34) | copy-start | bytes 540676
  172.8 91.2 %copy-start.6 = (bf16[128,4096]{1,0:T(8,128)(2,1)S(1)}, bf16[128,4096]{1,0:T(8,128)(2,1)}, u32[]{:S(2)}) copy-start(bf16[128,4096]{1,0:T(8,128)(2,1)} %param.20) | copy-start | bytes 3145732
  172.8 92.7 %copy-start.16 = (bf16[2048,128]{1,0:T(8,128)(2,1)S(1)}, bf16[2048,128]{1,0:T(8,128)(2,1)}, u32[]{:S(2)}) copy-start(bf16[2048,128]{1,0:T(8,128)(2,1)} %param.29) | copy-start | bytes 1572868
  248.6 15.2 %all-to-all-start.2 = ((bf16[16,2,2,4096]{3,2,1,0:T(2,128)(2,1)}), bf16[16,2,2,4096]{3,2,1,0:T(2,128)(2,1)S(1)}, u32[]{:S(2)}, u32[]{:S(2)}) async-start(bf16[16,2,2,4096]{3,2,1,0:T(2,128)(2,1)} %reshape.304), calls=%async_computation.3 | async-start | bytes 1048576 | tf_op jit(solution)/shard_map/all_to_all | solution.py:204
  253.0 101.4 %all-gather.10.cloned.1.call-start = ((), (), s32[]{:S(2)}) async-start(), calls=%async_computation.10 | async-start | bytes 17825792 | tf_op jit(solution)/shard_map/all_gather | solution.py:221
  265.5 174.1 %all-gather.14.cloned.1.call-start = ((), (), s32[]{:S(2)}) async-start(), calls=%async_computation.13 | async-start | bytes 4718592 | tf_op jit(solution)/shard_map/all_gather | solution.py:236
  366.8 144.3 %all-gather.12.cloned.1.call-start = ((), (), s32[]{:S(2)}) async-start(), calls=%async_computation.12 | async-start | bytes 4718592 | tf_op jit(solution)/shard_map/all_gather | solution.py:235
  367.4 441.0 %reduce-scatter.13.cloned.1.call-start = ((), (), s32[]{:S(2)}) async-start(), calls=%async_computation.15 | async-start | bytes 36864
  368.9 440.8 %reduce-scatter.9.cloned.1.call-start = ((), (), s32[]{:S(2)}) async-start(), calls=%async_computation.11 | async-start | bytes 1179648 | tf_op jit(solution)/shard_map/reduce_scatter | solution.py:226
  414.6 465.8 %reduce-scatter.11.cloned.1.call-start = ((), (), s32[]{:S(2)}) async-start(), calls=%async_computation.14 | async-start | bytes 4718592 | tf_op jit(solution)/shard_map/reduce_scatter | solution.py:242
  446.0 67.4 %copy-start.7 = (bf16[2048,128]{1,0:T(8,128)(2,1)S(1)}, bf16[2048,128]{1,0:T(8,128)(2,1)}, u32[]{:S(2)}) copy-start(bf16[2048,128]{1,0:T(8,128)(2,1)} %param.27) | copy-start | bytes 1572868
  529.0 6.2 copy-start.23
  562.2 6.2 copy-start.23
  596.9 6.2 copy-start.23
  666.2 6.2 copy-start.23
  803.3 77.2 %copy-start.1 = (bf16[2,4096,176]{1,2,0:T(8,128)(2,1)S(1)}, bf16[2,4096,176]{1,2,0:T(8,128)(2,1)}, u32[]{:S(2)}) copy-start(bf16[2,4096,176]{1,2,0:T(8,128)(2,1)} %param.21) | copy-start | bytes 8650756
  (27 other events, 124.1 us)
Sparse Core Ops, SparseCore 0:
  56.8 53.7 all-gather.7
  113.5 51.8 all-gather.5
  172.9 72.9 reduce-scatter.6
  265.6 88.7 all-gather.9
  366.9 72.5 all-gather.13
  441.8 69.3 all-gather.11
  514.5 59.8 reduce-scatter.12
  578.0 70.7 reduce-scatter.8
  799.3 81.0 reduce-scatter.10
where the time goes:
time: 898 us; the launch traced here: 887 us
  waiting for transfers between devices  450 us (50%)
  matrix products  258 us (29%)
  local copies, waits for them, and re-layouts  61.6 us (7%)
  blocking collectives  36.5 us (4%)
  other arithmetic  35.8 us (4%)
  loops' own time  15.8 us (2%)
  starting transfers between devices  14.9 us (2%)
  between operations  14.5 us (2%)
    dot_general x17, matrix products, contract_first(): lax.dot_general(left, right, (((0,), (0,)), ((), ())), preferred_element_...  107 us
    dot_general x17, matrix products, contract_last(): lax.dot_general(left, right, (((1,), (1,)), ((), ())), preferred_element_...  106 us
    all_gather x1, waiting for transfers between devices, body(): piece_rows = lax.all_gather(d_resid, 'exp', axis=0, tiled=True)  88.6 us
    reduce_scatter x1, waiting for transfers between devices, body(): lax.psum_scatter(dx_part.astype(jnp.bfloat16), 'ctx', scatter_dimension=1...  73 us
    all_gather x1, waiting for transfers between devices, body(): q_rows = lax.all_gather(queries, 'ctx', axis=0, tiled=True)  65.2 us
    reduce_scatter x1, waiting for transfers between devices, body(): lax.psum_scatter(dq_all.astype(jnp.bfloat16), 'ctx', scatter_dimension=0,...  64.9 us
    all_gather x1, waiting for transfers between devices, body(): lax.all_gather(mine_rows, 'ctx', axis=1, tiled=True)  52.4 us
    all_gather x1, waiting for transfers between devices, body(): lax.all_gather(mine_grads, 'ctx', axis=1, tiled=True)  50.8 us
  transfers between devices with their start and end apart: 12, of which 10 were waited for; matrix products, arithmetic and copies ran while one was open for 35% of the time, Pallas kernels for 0%

commit v1 on v0

--- a/solution.py
+++ b/solution.py
@@ -5,6 +5,18 @@
 from jax.sharding import PartitionSpec as P
 
 MOST = 2
+
+
+def treat_lane_on(vals, row_axis, axis_no):
+    return jnp.concatenate(
+        jax.lax.all_to_all(
+            jnp.stack([vals for _ in range(jax.lax.axis_size(row_axis))], axis=0),
+            axis_name=row_axis,
+            split_axis=0,
+            concat_axis=0,
+        ),
+        axis=axis_no,
+    )
 
 
 def activation(pre_act):
@@ -218,7 +230,7 @@
     ).astype(jnp.bfloat16)
     tok_ctx, head_dim = queries.shape
     key_scale = head_dim ** (-0.5)
-    piece_rows = lax.all_gather(d_resid, "exp", axis=0, tiled=True)
+    piece_rows = treat_lane_on(d_resid, "exp", 0)
     out_rows = contract_last(piece_rows, w_out)
     d_out_acc = out_rows.astype(jnp.bfloat16)
     dw_part = contract_first(attn_out, piece_rows)

time: 898 us -> 1050 us (1.17)
  waiting for transfers between devices: 450 us -> 584 us
    all_to_all x0 -> x1, waiting for transfers between devices: none -> 224 us  [treat_lane_on(): jax.lax.all_to_all(jnp.stack([vals for _ in range(jax.lax.axis_size(row_a...]
    all_gather x1 -> x0, waiting for transfers between devices: 88.6 us -> none  [body(): piece_rows = lax.all_gather(d_resid, 'exp', axis=0, tiled=True)]
    dot_general x8, matrix products: 27 us -> 54.9 us  [compute_tile(): jnp.dot(d_scores, keys_piece, preferred_element_type=jnp.float32)]
    dot_general x17, matrix products: 107 us -> 85.9 us  [contract_first(): lax.dot_general(left, right, (((0,), (0,)), ((), ())), preferred_element_...]
  transfers between devices with their start and end apart: 12 -> 12, of which waited for: 10 -> 10; matrix products, arithmetic and copies ran while one was open for 35% -> 31% of each run, Pallas kernels for 0% -> 0%
where the time goes in v1:
time: 1050 us; the launch traced here: 1040 us
  waiting for transfers between devices  584 us (56%)
  matrix products  266 us (25%)
  local copies, waits for them, and re-layouts  68 us (6%)
  blocking collectives  35.7 us (3%)
  other arithmetic  35.6 us (3%)
  starting transfers between devices  20.1 us (2%)
  loops' own time  15.3 us (1%)
  between operations  14.8 us (1%)
    all_to_all x1, waiting for transfers between devices, treat_lane_on(): jax.lax.all_to_all(jnp.stack([vals for _ in range(jax.lax.axis_size(row_a...  224 us
    dot_general x17, matrix products, contract_last(): lax.dot_general(left, right, (((1,), (1,)), ((), ())), preferred_element_...  107 us
    dot_general x17, matrix products, contract_first(): lax.dot_general(left, right, (((0,), (0,)), ((), ())), preferred_element_...  85.9 us
    reduce_scatter x1, waiting for transfers between devices, body(): lax.psum_scatter(dx_part.astype(jnp.bfloat16), 'ctx', scatter_dimension=1...  73 us
    all_gather x1, waiting for transfers between devices, body(): q_rows = lax.all_gather(queries, 'ctx', axis=0, tiled=True)  65.2 us
    reduce_scatter x1, waiting for transfers between devices, body(): lax.psum_scatter(dq_all.astype(jnp.bfloat16), 'ctx', scatter_dimension=0,...  64.8 us
    dot_general x8, matrix products, compute_tile(): jnp.dot(d_scores, keys_piece, preferred_element_type=jnp.float32)  54.9 us
    all_gather x1, waiting for transfers between devices, body(): lax.all_gather(mine_rows, 'ctx', axis=1, tiled=True)  52.4 us
  transfers between devices with their start and end apart: 12, of which 10 were waited for; matrix products, arithmetic and copies ran while one was open for 31% of the time, Pallas kernels for 0%

profile of v1, /device:TPU:0, one launch (start us, length us, event | category | flops | bytes accessed | tf_op | source)
XLA Modules:
  0.0 1040.1 jit_solution(9660725704020494511)
XLA Ops:
  26.4 10.5 %all-to-all-done = bf16[16,2,2,4096]{3,2,1,0:T(2,128)(2,1)S(1)} async-done(((bf16[16,2,2,4096]{3,2,1,0:T(2,128)(2,1)}), bf16[16,2,2,4096]{3,2,1,0:T(2,128)(2,1)S(1)}, u32[]{:S(2)}, u32[]{:S(2)}) %all-to-all-start) | async-done | bytes 524320 | tf_op jit(solution)/shard_map/all_to_all | solution.py:148
  58.2 52.4 %all-gather.7.cloned.1.call-done = bf16[2,128,4096]{2,1,0:T(8,128)(2,1)} async-done(((bf16[2,16,4096]{2,1,0:T(8,128)(2,1)}), bf16[2,128,4096]{2,1,0:T(8,128)(2,1)}) %all-gather.7.cloned.1.call-update) | async-done | bytes 2097168 | tf_op jit(solution)/shard_map/all_gather | solution.py:174
  115.1 50.3 %all-gather.5.cloned.1.call-done = bf16[2,128,4096]{2,1,0:T(8,128)(2,1)} async-done(((bf16[2,16,4096]{2,1,0:T(8,128)(2,1)}), bf16[2,128,4096]{2,1,0:T(8,128)(2,1)}) %all-gather.5.cloned.1.call-update) | async-done | bytes 2097168 | tf_op jit(solution)/shard_map/all_gather | solution.py:175
  172.9 73.0 %reduce-scatter.7.cloned.1.call-done = bf16[2,16,4096]{2,1,0:T(8,128)(2,1)} async-done(((bf16[2,128,4096]{2,1,0:T(8,128)(2,1)}), bf16[2,16,4096]{2,1,0:T(8,128)(2,1)}) %reduce-scatter.7.cloned.1.call-update) | async-done | bytes 262160 | tf_op jit(solution)/shard_map/reduce_scatter | solution.py:203
  253.8 10.4 all-to-all-done.2
  277.3 224.4 %all-to-all-done.3 = bf16[16,128,4096]{2,1,0:T(8,128)(2,1)} async-done(((bf16[16,128,4096]{2,1,0:T(8,128)(2,1)}), bf16[16,128,4096]{2,1,0:T(8,128)(2,1)}, u32[]{:S(2)}, u32[]{:S(2)}) %all-to-all-start.3) | async-done | bytes 16777248 | tf_op jit(solution)/shard_map/all_to_all | solution.py:12
  501.7 12.2 %multiply_reduce_fusion = (f32[2048]{0:T(1024)S(1)}, bf16[2048,128]{0,1:T(8,128)(2,1)}) fusion(bf16[2048,128]{0,1:T(8,128)(2,1)S(1)} %copy.31, bf16[2048,4096]{1,0:T(8,128)(2,1)} %bitcast.4, bf16[128,4096]{1,0:T(8,128)(2,1)S(1)} %copy-done.25), kind=kOutput, calls=%fused_computation.41 | convolution fusion | flops 2148792320 | bytes 18882560 | tf_op jit(solution)/shard_map/dot_general | solution.py:38
  516.0 9.2 fusion.18
  525.2 35.7 %all_gather.19 = f32[16384]{0:T(1024)} all-gather(f32[2048]{0:T(1024)S(1)} %get-tuple-element.634), channel_id=1, replica_groups=mesh['ctx'=8,'exp'=16] {'ctx'}, dimensions={0}, use_global_device_ids=true | all-gather | bytes 73728 | tf_op jit(solution)/shard_map/all_gather | solution.py:246
  561.0 24.0 %all-gather.11.cloned.1.call-done = bf16[16384,128]{0,1:T(8,128)(2,1)} async-done(((bf16[2048,128]{0,1:T(8,128)(2,1)}), bf16[16384,128]{0,1:T(8,128)(2,1)}) %all-gather.11.cloned.1.call-update) | async-done | bytes 4194320 | tf_op jit(solution)/shard_map/all_gather | solution.py:248
  591.5 65.2 %all-gather.9.cloned.1.call-done = bf16[16384,128]{1,0:T(8,128)(2,1)} async-done(((bf16[2048,128]{1,0:T(8,128)(2,1)}), bf16[16384,128]{1,0:T(8,128)(2,1)}) %all-gather.9.cloned.1.call-update) | async-done | bytes 4194320 | tf_op jit(solution)/shard_map/all_gather | solution.py:247
  658.8 293.1 %while.22 = (s32[]{:T(128)}, bf16[16384,128]{1,0:T(8,128)(2,1)}, f32[2048,128]{1,0:T(8,128)}, f32[2048,128]{1,0:T(8,128)}, s32[]{:T(128)}, /*index=5*/bf16[16384...) while((s32[]{:T(128)}, bf16[16384,128]{1,0:T(8,128)(2,1)}, ...), condition=%wide.region_13.15_spmd.clone, body=%wide.region_10.14_spmd.clone.sunk | while | flops 5420617728 | bytes 126553064 | solution.py:100
  669.5 29.8 %conditional.3 = (f32[2048,128]{1,0:T(8,128)}, f32[2048,128]{1,0:T(8,128)S(1)}, f32[2048,128]{1,0:T(8,128)S(1)}) conditional(s32[]{:T(128)} %convert_element_type.156, () %tuple.94, (s32[]{:T(128)}, s32[]{:T(128)}, s32[2048]{0:T(1024)S(1)}, bf16[16384,128]{1,0:T(8,128)(2,1)}, s32[]{:T(128)}, /*index=5*/bf16[2048,128]{1,0:T(8,128)(2,1)S(1)}, ...), branch_computations={%region_11.12_spmd, %region_12.13_spmd} | conditional | flops 5419569152 | bytes 118155424 | solution.py:85
  703.6 29.8 %conditional.3 = (f32[2048,128]{1,0:T(8,128)}, f32[2048,128]{1,0:T(8,128)S(1)}, f32[2048,128]{1,0:T(8,128)S(1)}) conditional(s32[]{:T(128)} %convert_element_type.156, () %tuple.94, (s32[]{:T(128)}, s32[]{:T(128)}, s32[2048]{0:T(1024)S(1)}, bf16[16384,128]{1,0:T(8,128)(2,1)}, s32[]{:T(128)}, /*index=5*/bf16[2048,128]{1,0:T(8,128)(2,1)S(1)}, ...), branch_computations={%region_11.12_spmd, %region_12.13_spmd} | conditional | flops 5419569152 | bytes 118155424 | solution.py:85
  708.5 8.4 multiply_convert_fusion
  739.1 29.8 %conditional.3 = (f32[2048,128]{1,0:T(8,128)}, f32[2048,128]{1,0:T(8,128)S(1)}, f32[2048,128]{1,0:T(8,128)S(1)}) conditional(s32[]{:T(128)} %convert_element_type.156, () %tuple.94, (s32[]{:T(128)}, s32[]{:T(128)}, s32[2048]{0:T(1024)S(1)}, bf16[16384,128]{1,0:T(8,128)(2,1)}, s32[]{:T(128)}, /*index=5*/bf16[2048,128]{1,0:T(8,128)(2,1)S(1)}, ...), branch_computations={%region_11.12_spmd, %region_12.13_spmd} | conditional | flops 5419569152 | bytes 118155424 | solution.py:85
  744.0 8.4 multiply_convert_fusion
  774.7 29.8 %conditional.3 = (f32[2048,128]{1,0:T(8,128)}, f32[2048,128]{1,0:T(8,128)S(1)}, f32[2048,128]{1,0:T(8,128)S(1)}) conditional(s32[]{:T(128)} %convert_element_type.156, () %tuple.94, (s32[]{:T(128)}, s32[]{:T(128)}, s32[2048]{0:T(1024)S(1)}, bf16[16384,128]{1,0:T(8,128)(2,1)}, s32[]{:T(128)}, /*index=5*/bf16[2048,128]{1,0:T(8,128)(2,1)S(1)}, ...), branch_computations={%region_11.12_spmd, %region_12.13_spmd} | conditional | flops 5419569152 | bytes 118155424 | solution.py:85
  779.6 8.4 multiply_convert_fusion
  810.3 29.7 %conditional.3 = (f32[2048,128]{1,0:T(8,128)}, f32[2048,128]{1,0:T(8,128)S(1)}, f32[2048,128]{1,0:T(8,128)S(1)}) conditional(s32[]{:T(128)} %convert_element_type.156, () %tuple.94, (s32[]{:T(128)}, s32[]{:T(128)}, s32[2048]{0:T(1024)S(1)}, bf16[16384,128]{1,0:T(8,128)(2,1)}, s32[]{:T(128)}, /*index=5*/bf16[2048,128]{1,0:T(8,128)(2,1)S(1)}, ...), branch_computations={%region_11.12_spmd, %region_12.13_spmd} | conditional | flops 5419569152 | bytes 118155424 | solution.py:85
  845.8 29.7 %conditional.3 = (f32[2048,128]{1,0:T(8,128)}, f32[2048,128]{1,0:T(8,128)S(1)}, f32[2048,128]{1,0:T(8,128)S(1)}) conditional(s32[]{:T(128)} %convert_element_type.156, () %tuple.94, (s32[]{:T(128)}, s32[]{:T(128)}, s32[2048]{0:T(1024)S(1)}, bf16[16384,128]{1,0:T(8,128)(2,1)}, s32[]{:T(128)}, /*index=5*/bf16[2048,128]{1,0:T(8,128)(2,1)S(1)}, ...), branch_computations={%region_11.12_spmd, %region_12.13_spmd} | conditional | flops 5419569152 | bytes 118155424 | solution.py:85
  881.4 29.7 %conditional.3 = (f32[2048,128]{1,0:T(8,128)}, f32[2048,128]{1,0:T(8,128)S(1)}, f32[2048,128]{1,0:T(8,128)S(1)}) conditional(s32[]{:T(128)} %convert_element_type.156, () %tuple.94, (s32[]{:T(128)}, s32[]{:T(128)}, s32[2048]{0:T(1024)S(1)}, bf16[16384,128]{1,0:T(8,128)(2,1)}, s32[]{:T(128)}, /*index=5*/bf16[2048,128]{1,0:T(8,128)(2,1)S(1)}, ...), branch_computations={%region_11.12_spmd, %region_12.13_spmd} | conditional | flops 5419569152 | bytes 118155424 | solution.py:85
  916.9 29.7 %conditional.3 = (f32[2048,128]{1,0:T(8,128)}, f32[2048,128]{1,0:T(8,128)S(1)}, f32[2048,128]{1,0:T(8,128)S(1)}) conditional(s32[]{:T(128)} %convert_element_type.156, () %tuple.94, (s32[]{:T(128)}, s32[]{:T(128)}, s32[2048]{0:T(1024)S(1)}, bf16[16384,128]{1,0:T(8,128)(2,1)}, s32[]{:T(128)}, /*index=5*/bf16[2048,128]{1,0:T(8,128)(2,1)S(1)}, ...), branch_computations={%region_11.12_spmd, %region_12.13_spmd} | conditional | flops 5419569152 | bytes 118155424 | solution.py:85
  968.2 64.8 %reduce-scatter.11.cloned.1.call-done = bf16[2048,128]{1,0:T(8,128)(2,1)} async-done(((bf16[16384,128]{1,0:T(8,128)(2,1)}), bf16[2048,128]{1,0:T(8,128)(2,1)}) %reduce-scatter.11.cloned.1.call-update) | async-done | bytes 524304 | tf_op jit(solution)/shard_map/reduce_scatter | solution.py:254
  (282 shorter events, 352.8 us)
Async XLA Ops:
  7.2 107.0 %copy-start = (bf16[2,4096,176]{1,2,0:T(8,128)(2,1)S(1)}, bf16[2,4096,176]{1,2,0:T(8,128)(2,1)}, u32[]{:S(2)}) copy-start(bf16[2,4096,176]{1,2,0:T(8,128)(2,1)} %param.21) | copy-start | bytes 8650756
  20.6 16.4 %all-to-all-start = ((bf16[16,2,2,4096]{3,2,1,0:T(2,128)(2,1)}), bf16[16,2,2,4096]{3,2,1,0:T(2,128)(2,1)S(1)}, u32[]{:S(2)}, u32[]{:S(2)}) async-start(bf16[16,2,2,4096]{3,2,1,0:T(2,128)(2,1)} %get-tuple-element.630), calls=%async_computation | async-start | bytes 1048576 | tf_op jit(solution)/shard_map/all_to_all | solution.py:148
  36.9 15.1 %all-to-all-start.1 = ((bf16[16,2,2,4096]{3,2,1,0:T(2,128)(2,1)}), bf16[16,2,2,4096]{3,2,1,0:T(2,128)(2,1)}, u32[]{:S(2)}, u32[]{:S(2)}) async-start(bf16[16,2,2,4096]{3,2,1,0:T(2,128)(2,1)} %get-tuple-element.631), calls=%async_computation.1 | async-start | bytes 1048576 | tf_op jit(solution)/shard_map/all_to_all | solution.py:141
  41.2 69.4 %all-gather.7.cloned.1.call-start = ((), (), s32[]{:S(2)}) async-start(), calls=%async_computation.9 | async-start | bytes 2359296 | tf_op jit(solution)/shard_map/all_gather | solution.py:174
  56.7 108.7 %all-gather.5.cloned.1.call-start = ((), (), s32[]{:S(2)}) async-start(), calls=%async_computation.8 | async-start | bytes 2359296 | tf_op jit(solution)/shard_map/all_gather | solution.py:175
  57.4 188.5 %reduce-scatter.7.cloned.1.call-start = ((), (), s32[]{:S(2)}) async-start(), calls=%async_computation.10 | async-start | bytes 2359296 | tf_op jit(solution)/shard_map/reduce_scatter | solution.py:203
  58.2 107.2 %copy-start.23 = (f32[2,128]{1,0:T(2,128)}, f32[2,128]{1,0:T(2,128)S(1)}, u32[]{:S(2)}) copy-start(f32[2,128]{1,0:T(2,128)S(1)} %constant_dynamic-slice_fusion) | copy-start | bytes 3076
  114.1 54.6 %copy-start.12 = (f32[2,128,176]{1,2,0:T(8,128)}, f32[2,128,176]{1,2,0:T(8,128)S(1)}, u32[]{:S(2)}) copy-start(f32[2,128,176]{1,2,0:T(8,128)S(1)} %fusion.34) | copy-start | bytes 540676
  115.1 54.5 %copy-start.14 = (f32[2,128,176]{1,2,0:T(8,128)}, f32[2,128,176]{1,2,0:T(8,128)S(1)}, u32[]{:S(2)}) copy-start(f32[2,128,176]{1,2,0:T(8,128)S(1)} %fusion.35) | copy-start | bytes 540676
  172.8 91.6 %copy-start.6 = (bf16[128,4096]{1,0:T(8,128)(2,1)S(1)}, bf16[128,4096]{1,0:T(8,128)(2,1)}, u32[]{:S(2)}) copy-start(bf16[128,4096]{1,0:T(8,128)(2,1)} %param.20) | copy-start | bytes 3145732
  248.6 15.6 %all-to-all-start.2 = ((bf16[16,2,2,4096]{3,2,1,0:T(2,128)(2,1)}), bf16[16,2,2,4096]{3,2,1,0:T(2,128)(2,1)S(1)}, u32[]{:S(2)}, u32[]{:S(2)}) async-start(bf16[16,2,2,4096]{3,2,1,0:T(2,128)(2,1)} %reshape.309), calls=%async_computation.3 | async-start | bytes 1048576 | tf_op jit(solution)/shard_map/all_to_all | solution.py:216
  271.7 230.0 %copy-start.25 = (bf16[128,4096]{1,0:T(8,128)(2,1)S(1)}, bf16[128,4096]{1,0:T(8,128)(2,1)}, u32[]{:S(2)}) copy-start(bf16[128,4096]{1,0:T(8,128)(2,1)} %param.31) | copy-start | bytes 3145732
  271.7 230.0 %all-to-all-start.3 = ((bf16[16,128,4096]{2,1,0:T(8,128)(2,1)}), bf16[16,128,4096]{2,1,0:T(8,128)(2,1)}, u32[]{:S(2)}, u32[]{:S(2)}) async-start(bf16[16,128,4096]{2,1,0:T(8,128)(2,1)} %stack.2), calls=%async_computation.4 | async-start | bytes 33554432 | tf_op jit(solution)/shard_map/all_to_all | solution.py:12
  277.0 308.0 %all-gather.11.cloned.1.call-start = ((), (), s32[]{:S(2)}) async-start(), calls=%async_computation.13 | async-start | bytes 4718592 | tf_op jit(solution)/shard_map/all_gather | solution.py:248
  513.9 142.7 %all-gather.9.cloned.1.call-start = ((), (), s32[]{:S(2)}) async-start(), calls=%async_computation.12 | async-start | bytes 4718592 | tf_op jit(solution)/shard_map/all_gather | solution.py:247
  514.5 446.6 %reduce-scatter.13.cloned.1.call-start = ((), (), s32[]{:S(2)}) async-start(), calls=%async_computation.15 | async-start | bytes 36864
  515.9 446.5 %reduce-scatter.9.cloned.1.call-start = ((), (), s32[]{:S(2)}) async-start(), calls=%async_computation.11 | async-start | bytes 1179648 | tf_op jit(solution)/shard_map/reduce_scatter | solution.py:238
  561.0 472.1 %reduce-scatter.11.cloned.1.call-start = ((), (), s32[]{:S(2)}) async-start(), calls=%async_computation.14 | async-start | bytes 4718592 | tf_op jit(solution)/shard_map/reduce_scatter | solution.py:254
  591.5 67.4 %copy-start.7 = (bf16[2048,128]{1,0:T(8,128)(2,1)S(1)}, bf16[2048,128]{1,0:T(8,128)(2,1)}, u32[]{:S(2)}) copy-start(bf16[2048,128]{1,0:T(8,128)(2,1)} %param.27) | copy-start | bytes 1572868
  708.5 8.4 copy-start.21
  744.0 8.4 copy-start.21
  779.6 8.4 copy-start.21
  850.7 8.4 copy-start.21
  956.0 77.1 %copy-start.1 = (bf16[2,4096,176]{1,2,0:T(8,128)(2,1)S(1)}, bf16[2,4096,176]{1,2,0:T(8,128)(2,1)}, u32[]{:S(2)}) copy-start(bf16[2,4096,176]{1,2,0:T(8,128)(2,1)} %param.21) | copy-start | bytes 8650756
  (44 other events, 210.6 us)
Sparse Core Ops, SparseCore 0:
  56.8 53.7 all-gather.6
  113.5 51.8 all-gather.4
  172.9 72.9 reduce-scatter.6
  514.0 70.9 all-gather.10
  587.3 69.3 all-gather.8
  659.8 59.8 reduce-scatter.12
  723.3 70.7 reduce-scatter.8
  952.0 80.9 reduce-scatter.10
